TPU v7x, 32 devices: a whole 2x2x4 slice. The times are simulated.
32 devices in a mesh: branch: 8 (over y, x, core), mode: 4 (over z).
Axes of the slice: x: 2, y: 2, z: 4, core: 2. Of those that a mesh axis runs over, the one named last changes fastest.
Arguments:
- stem: float32 [2, 8, 512, 4, 512], P(None, 'branch', None, 'mode'), may hold values from -6 to 6
- left_factors: bfloat16 [2, 2, 8, 512, 512], P(None, None, 'branch', 'mode'), may hold values from -0.1875 to 0.1875
- right_factors: bfloat16 [2, 2, 8, 512, 512], P(None, None, 'branch', 'mode'), may hold values from -0.1875 to 0.1875
- owners: int32 [2], replicated, may hold values from 0 to 7
Outputs:
- contracted: float32 [2, 8, 512, 4, 512], P(None, 'branch', None, 'mode')
All inputs are finite; a program needn't handle non-finite values.
Results may differ from a plain program's by a relative error of at most 0.0003.
Values may be sent and summed in bfloat16 or wider, within the bound.
No kernel may reach another device: no remote copies, remote signals or barrier semaphores. Data moves between devices by JAX's collectives and lax.ppermute only.
A program may use at most 64 MiB of HBM per device.

v0:
```python
import jax
import jax.numpy as jnp
from jax import lax
from jax.sharding import PartitionSpec as P


def spread(block, axis, holder):
    block = jnp.where(lax.axis_index(axis) == holder, block, jnp.zeros_like(block))
    return lax.psum(block, axis)


def complex_apply(field_re, field_im, branch):
    high = lax.Precision.HIGHEST
    real_part = jnp.dot(field_re, branch[0], precision=high) - jnp.dot(
        field_im, branch[1], precision=high
    )
    imag_part = jnp.dot(field_re, branch[1], precision=high) + jnp.dot(
        field_im, branch[0], precision=high
    )
    return (real_part, imag_part)


def shards(stem, left_factors, right_factors, owners):
    width = stem.shape[4]

    def form_branch(which):
        left = left_factors[which, :, 0]
        right = right_factors[which]
        piece = lax.all_gather(right, "mode", axis=2, tiled=True)
        real_part = jnp.dot(left[0], piece[0, 0], preferred_element_type=jnp.float32) - jnp.dot(
            left[1], piece[1, 0], preferred_element_type=jnp.float32
        )
        imag_part = jnp.dot(left[0], piece[1, 0], preferred_element_type=jnp.float32) + jnp.dot(
            left[1], piece[0, 0], preferred_element_type=jnp.float32
        )
        formed = jnp.stack([real_part, imag_part])
        holder = owners[which]
        received = spread(formed, "branch", holder)
        return lax.all_gather(received, "mode", axis=1, tiled=True)

    first_branch = form_branch(0)
    second_branch = form_branch(1)
    real_one, imag_one = complex_apply(stem[0, 0, :, 0, :], stem[1, 0, :, 0, :], first_branch)
    outgoing = jnp.stack([real_one, imag_one])[:, None, :, None, :]
    arrived = lax.all_to_all(outgoing, "mode", split_axis=4, concat_axis=3, tiled=True)
    count = arrived.shape[2]
    merged = arrived.reshape(2, count, width)
    real_two, imag_two = complex_apply(merged[0], merged[1], second_branch)
    return jnp.stack([real_two, imag_two])[:, None, :, None, :]


def solution(mesh):
    placed = (
        P(None, "branch", None, "mode", None),
        P(None, None, "branch", "mode", None),
        P(None, None, "branch", "mode", None),
        P(),
    )
    return jax.shard_map(
        shards,
        mesh=mesh,
        in_specs=placed,
        out_specs=P(None, "branch", None, "mode", None),
        check_vma=False,
    )
```

profile of v0, /device:TPU:0, one launch (start us, length us, event | category | flops | bytes accessed | tf_op | source)
XLA Modules:
  0.0 303.5 jit_solution(10032876281530875387)
XLA Ops:
  6.5 0.0 all-gather.11.cloned.1.call-start
  6.5 1.9 fusion.50
  8.4 0.0 all-gather.11.cloned.1.call-update
  8.5 0.0 all-gather.13.cloned.1.call-start
  8.5 0.7 all-gather.13.cloned.1.call-update
  9.2 0.0 all-reduce.3.cloned.1.call-start
  9.3 1.3 fusion.51
  11.9 27.8 %all-gather.11.cloned.1.call-done = bf16[1,2,1,512,512]{4,3,2,1,0:T(8,128)(2,1)} async-done(((bf16[1,2,1,128,512]{4,3,2,1,0:T(8,128)(2,1)}), bf16[1,2,1,512,512]{4,3,2,1,0:T(8,128)(2,1)}) %all-gather.11.cloned.1.call-update) | async-done | bytes 1048592 | tf_op jit(solution)/shard_map/all_gather | solution.py:29
  39.6 1.4 fusion.29
  41.1 0.0 copy-done.4
  41.1 1.3 fusion.6
  42.4 0.0 copy-done.3
  42.4 0.2 fusion.28
  42.6 0.2 fusion.7
  42.8 0.8 maximum_select_fusion
  43.7 24.9 %all-gather.13.cloned.1.call-done = bf16[1,2,1,512,512]{4,3,2,1,0:T(8,128)(2,1)} async-done(((bf16[1,2,1,128,512]{4,3,2,1,0:T(8,128)(2,1)}), bf16[1,2,1,512,512]{4,3,2,1,0:T(8,128)(2,1)}) %all-gather.13.cloned.1.call-update) | async-done | bytes 1048592 | tf_op jit(solution)/shard_map/all_gather | solution.py:29
  68.6 1.4 fusion.30
  70.0 1.3 fusion.31
  71.3 0.0 copy-done.2
  71.3 0.2 fusion.5
  71.5 0.2 fusion.4
  71.8 0.8 maximum_select_fusion.1
  72.6 0.0 all-reduce.3.cloned.1.call-update
  72.6 0.0 all-gather.7.cloned.1.call-start
  72.7 56.3 %all-reduce.3.cloned.1.call-done = (f32[2,128,512]{2,1,0:T(8,128)}, f32[2,128,512]{2,1,0:T(8,128)}) async-done(((f32[2,128,512]{2,1,0:T(8,128)}, f32[2,128,512]{2,1,0:T(8,128)}), (f32[2,128,512]{2,1,0:T(8,128)}, f32[2,128,512]{2,1,0:T(8,128)})) %all-reduce.3.cloned.1.call-update) | async-done | bytes 1048592 | tf_op jit(solution)/shard_map/psum | solution.py:9
  128.9 0.0 all-gather.7.cloned.1.call-update
  129.0 3.0 fusion.49
  131.9 43.4 %all-gather.7.cloned.1.call-done = f32[2,512,512]{2,1,0:T(8,128)} async-done(((f32[2,128,512]{2,1,0:T(8,128)}), f32[2,512,512]{2,1,0:T(8,128)}) %all-gather.7.cloned.1.call-update) | async-done | bytes 2097168 | tf_op jit(solution)/shard_map/all_gather | solution.py:39
  175.3 4.8 %fusion.18 = f32[512,512]{1,0:T(8,128)S(1)} fusion(f32[2,512,512]{2,1,0:T(8,128)} %all-gather.7.cloned.1.call-done, f32[1,1,512,1,512]{4,3,2,1,0:T(1,128)S(1)} %get-tuple-element.10), kind=kOutput, calls=%fused_computation.32 | convolution fusion | flops 1610612736 | bytes 3145728 | tf_op jit(solution)/shard_map/dot_general | solution.py:14
  180.2 0.0 copy-done.1
  180.2 3.5 %fusion.16 = f32[512,512]{1,0:T(8,128)S(1)} fusion(f32[2,512,512]{2,1,0:T(8,128)S(1)} %copy-done.1, f32[1,1,512,1,512]{4,3,2,1,0:T(1,128)S(1)} %get-tuple-element.10), kind=kOutput, calls=%fused_computation.30 | convolution fusion | flops 1610612736 | bytes 3145728 | tf_op jit(solution)/shard_map/dot_general | solution.py:17
  183.7 3.5 %fusion.3 = f32[1,512,512]{1,2,0:T(8,128)S(1)} fusion(f32[512,512]{1,0:T(8,128)S(1)} %fusion.18, f32[2,512,512]{2,1,0:T(8,128)S(1)} %copy-done.1, f32[1,1,512,1,512]{4,3,2,1,0:T(1,128)S(1)} %get-tuple-element.9), kind=kOutput, calls=%fused_computation.9 | convolution fusion | flops 1610874880 | bytes 4194304 | tf_op jit(solution)/shard_map/dot_general | solution.py:14
  187.1 3.7 %fusion.2 = f32[1,512,512]{1,2,0:T(8,128)S(1)} fusion(f32[512,512]{1,0:T(8,128)S(1)} %fusion.16, f32[2,512,512]{2,1,0:T(8,128)S(1)} %copy-done.1, f32[1,1,512,1,512]{4,3,2,1,0:T(1,128)S(1)} %get-tuple-element.9), kind=kOutput, calls=%fused_computation.7 | convolution fusion | flops 1610874880 | bytes 4194304 | tf_op jit(solution)/shard_map/dot_general | solution.py:17
  190.8 0.2 maximum_bitcast_fusion
  191.0 2.9 copy.6
  193.9 4.4 %all-to-all-start = ((f32[2,1,512,1,512]{2,0,3,1,4:T(2,128)}), f32[2,1,512,1,512]{2,0,3,1,4:T(2,128)}, u32[]{:S(2)}, u32[]{:S(2)}) async-start(f32[2,1,512,1,512]{2,0,3,1,4:T(2,128)} %copy.6), calls=%async_computation | async-start | bytes 4194304 | tf_op jit(solution)/shard_map/all_to_all | solution.py:45
  198.4 0.0 all-gather.9.cloned.1.call-start
  198.4 0.5 all-gather.9.cloned.1.call-update
  199.0 81.5 %all-to-all-done = f32[2,1,512,1,512]{2,0,3,1,4:T(2,128)} async-done(((f32[2,1,512,1,512]{2,0,3,1,4:T(2,128)}), f32[2,1,512,1,512]{2,0,3,1,4:T(2,128)}, u32[]{:S(2)}, u32[]{:S(2)}) %all-to-all-start) | async-done | bytes 2097184 | tf_op jit(solution)/shard_map/all_to_all | solution.py:45
  280.5 4.0 %fusion.48 = (f32[1,1,512,1,512]{2,0,3,1,4:T(1,128)S(1)}, f32[1,1,512,1,512]{2,0,3,1,4:T(1,128)S(1)}) fusion(f32[2,1,512,1,512]{2,0,3,1,4:T(2,128)} %all-to-all-done), kind=kLoop, calls=%fused_computation.68 | loop fusion | bytes 4194304 | tf_op jit(solution)/shard_map/slice | solution.py:48
  284.5 0.0 all-gather.9.cloned.1.call-done
  284.5 0.0 copy-start
  284.5 3.2 %fusion.12 = f32[512,512]{1,0:T(8,128)S(1)} fusion(f32[2,512,512]{2,1,0:T(8,128)} %all-gather.9.cloned.1.call-done, f32[1,1,512,1,512]{2,0,3,1,4:T(1,128)S(1)} %get-tuple-element.8), kind=kOutput, calls=%fused_computation.26 | convolution fusion | flops 1610612736 | bytes 3145728 | tf_op jit(solution)/shard_map/dot_general | solution.py:14
  287.8 1.9 fusion.10
  289.6 1.9 fusion.1
  291.5 1.9 fusion
  293.3 0.2 maximum_bitcast_fusion.1
  293.5 3.5 %copy.7 = f32[2,1,512,1,512]{4,3,2,1,0:T(1,128)} copy(f32[2,1,512,1,512]{4,2,0,3,1:T(8,128)S(1)} %maximum_bitcast_fusion.1) | data formatting | bytes 4194304 | tf_op jit(solution)/shard_map/broadcast_in_dim | solution.py:49
  (5 shorter events, 0.0 us)
Async XLA Ops:
  6.5 34.5 %copy-start.4 = (bf16[2,2,1,128,512]{4,3,2,1,0:T(8,128)(2,1)S(1)}, bf16[2,2,1,128,512]{4,3,2,1,0:T(8,128)(2,1)}, u32[]{:S(2)}) copy-start(bf16[2,2,1,128,512]{4,3,2,1,0:T(8,128)(2,1)} %param.5) | copy-start | bytes 1572868
  6.5 33.1 %all-gather.11.cloned.1.call-start = ((), (), s32[]{:S(2)}) async-start(), calls=%async_computation.3 | async-start | bytes 1310720 | tf_op jit(solution)/shard_map/all_gather | solution.py:29
  8.5 60.2 %all-gather.13.cloned.1.call-start = ((), (), s32[]{:S(2)}) async-start(), calls=%async_computation.4 | async-start | bytes 1310720 | tf_op jit(solution)/shard_map/all_gather | solution.py:29
  9.2 119.7 %all-reduce.3.cloned.1.call-start = ((), (), s32[]{:S(2)}) async-start(), calls=%async_computation.5 | async-start | bytes 2097152 | tf_op jit(solution)/shard_map/psum | solution.py:9
  39.6 2.7 copy-start.3
  68.6 2.6 copy-start.2
  72.6 102.7 %all-gather.7.cloned.1.call-start = ((), (), s32[]{:S(2)}) async-start(), calls=%async_computation.1 | async-start | bytes 2621440 | tf_op jit(solution)/shard_map/all_gather | solution.py:39
  175.3 4.9 %copy-start.1 = (f32[2,512,512]{2,1,0:T(8,128)S(1)}, f32[2,512,512]{2,1,0:T(8,128)}, u32[]{:S(2)}) copy-start(f32[2,512,512]{2,1,0:T(8,128)} %all-gather.7.cloned.1.call-done) | copy-start | bytes 6291460
  193.9 86.5 %all-to-all-start = ((f32[2,1,512,1,512]{2,0,3,1,4:T(2,128)}), f32[2,1,512,1,512]{2,0,3,1,4:T(2,128)}, u32[]{:S(2)}, u32[]{:S(2)}) async-start(f32[2,1,512,1,512]{2,0,3,1,4:T(2,128)} %copy.6), calls=%async_computation | async-start | bytes 4194304 | tf_op jit(solution)/shard_map/all_to_all | solution.py:45
  198.4 86.1 %all-gather.9.cloned.1.call-start = ((), (), s32[]{:S(2)}) async-start(), calls=%async_computation.2 | async-start | bytes 2621440 | tf_op jit(solution)/shard_map/all_gather | solution.py:39
  284.5 3.2 %copy-start = (f32[2,512,512]{2,1,0:T(8,128)S(1)}, f32[2,512,512]{2,1,0:T(8,128)}, u32[]{:S(2)}) copy-start(f32[2,512,512]{2,1,0:T(8,128)} %all-gather.9.cloned.1.call-done) | copy-start | bytes 6291460
Sparse Core Ops, SparseCore 0:
  8.9 30.6 all-gather.10
  41.2 27.3 all-gather.12
  72.7 56.1 all-reduce.2
  130.4 44.9 all-gather.6
  200.4 74.5 all-gather.8
where the time goes:
time: 304 us
  waiting for transfers between devices  235 us (77%)
  matrix products  30.5 us (10%)
  local copies, waits for them, and re-layouts  16.7 us (5%)
  between operations  14.6 us (5%)
  starting transfers between devices  4.61 us (2%)
    all_to_all x1, waiting for transfers between devices, shards(): lax.all_to_all(outgoing, 'mode', split_axis=4, concat_axis=3, tiled=True)  81.5 us
    psum x1, waiting for transfers between devices, spread(): return lax.psum(block, axis)  56.3 us
    all_gather x2, waiting for transfers between devices, form_branch(): piece = lax.all_gather(right, 'mode', axis=2, tiled=True)  52.7 us
    all_gather x2, waiting for transfers between devices, form_branch(): return lax.all_gather(received, 'mode', axis=1, tiled=True)  43.4 us
    dot_general x2, matrix products, complex_apply(): jnp.dot(field_re, branch[0], precision=high)  8.07 us
  transfers between devices with their start and end apart: 6, of which 5 were waited for; matrix products, arithmetic and copies ran while one was open for 4% of the time, Pallas kernels for 0%

commit v1 on v0

--- a/solution.py
+++ b/solution.py
@@ -36,7 +36,9 @@
         formed = jnp.stack([real_part, imag_part])
         holder = owners[which]
         received = spread(formed, "branch", holder)
-        return lax.all_gather(received, "mode", axis=1, tiled=True)
+        return jnp.concatenate(
+            lax.all_to_all(jnp.stack([received] * lax.axis_size("mode")), "mode", 0, 0), axis=1
+        )
 
     first_branch = form_branch(0)
     second_branch = form_branch(1)

time: 304 us -> 310 us (1.020)
  waiting for transfers between devices: 235 us -> 182 us
  blocking collectives: 0 us -> 52 us
  local copies, waits for them, and re-layouts: 16.7 us -> 23.1 us
  starting transfers between devices: 4.61 us -> 8.15 us
    all_to_all x0 -> x1, blocking collectives: none -> 52 us  [form_branch(): lax.all_to_all(jnp.stack([received] * lax.axis_size('mode')), 'mode', 0, 0)]
    all_gather x2 -> x0, waiting for transfers between devices: 43.4 us -> none  [form_branch(): return lax.all_gather(received, 'mode', axis=1, tiled=True)]
    all_to_all x1, waiting for transfers between devices: 81.5 us -> 46 us  [shards(): lax.all_to_all(outgoing, 'mode', split_axis=4, concat_axis=3, tiled=True)]
    all_to_all x0 -> x1, waiting for transfers between devices: none -> 26.3 us  [form_branch(): lax.all_to_all(jnp.stack([received] * lax.axis_size('mode')), 'mode', 0, 0)]
    all_to_all x0 -> x1, starting transfers between devices: none -> 3.61 us  [form_branch(): lax.all_to_all(jnp.stack([received] * lax.axis_size('mode')), 'mode', 0, 0)]
  transfers between devices with their start and end apart: 6 -> 5, of which waited for: 5 -> 5; matrix products, arithmetic and copies ran while one was open for 4% -> 9% of each run, Pallas kernels for 0% -> 0%
where the time goes in v1:
time: 310 us
  waiting for transfers between devices  182 us (59%)
  blocking collectives  52 us (17%)
  matrix products  28.1 us (9%)
  local copies, waits for them, and re-layouts  23.1 us (7%)
  between operations  14.6 us (5%)
  starting transfers between devices  8.15 us (3%)
    psum x1, waiting for transfers between devices, spread(): return lax.psum(block, axis)  56.3 us
    all_gather x2, waiting for transfers between devices, form_branch(): piece = lax.all_gather(right, 'mode', axis=2, tiled=True)  52.7 us
    all_to_all x1, blocking collectives, form_branch(): lax.all_to_all(jnp.stack([received] * lax.axis_size('mode')), 'mode', 0, 0)  52 us
    all_to_all x1, waiting for transfers between devices, shards(): lax.all_to_all(outgoing, 'mode', split_axis=4, concat_axis=3, tiled=True)  46 us
    all_to_all x1, waiting for transfers between devices, form_branch(): lax.all_to_all(jnp.stack([received] * lax.axis_size('mode')), 'mode', 0, 0)  26.3 us
  transfers between devices with their start and end apart: 5, of which 5 were waited for; matrix products, arithmetic and copies ran while one was open for 9% of the time, Pallas kernels for 0%

profile of v1, /device:TPU:0, one launch (start us, length us, event | category | flops | bytes accessed | tf_op | source)
XLA Modules:
  0.0 309.9 jit_solution(14430087132913416663)
XLA Ops:
  6.5 0.0 all-gather.5.cloned.1.call-start
  6.5 1.9 fusion.52
  8.4 0.0 all-gather.5.cloned.1.call-update
  8.5 0.0 all-gather.7.cloned.1.call-start
  8.5 0.7 all-gather.7.cloned.1.call-update
  9.2 0.0 all-reduce.3.cloned.1.call-start
  9.3 1.4 fusion.53
  11.9 27.7 %all-gather.5.cloned.1.call-done = bf16[1,2,1,512,512]{4,3,2,1,0:T(8,128)(2,1)} async-done(((bf16[1,2,1,128,512]{4,3,2,1,0:T(8,128)(2,1)}), bf16[1,2,1,512,512]{4,3,2,1,0:T(8,128)(2,1)}) %all-gather.5.cloned.1.call-update) | async-done | bytes 1048592 | tf_op jit(solution)/shard_map/all_gather | solution.py:29
  39.6 1.4 fusion.29
  41.1 0.0 copy-done.4
  41.1 1.3 fusion.6
  42.4 0.0 copy-done.3
  42.4 0.2 fusion.28
  42.6 0.2 fusion.7
  42.8 0.8 maximum_select_fusion
  43.7 25.0 %all-gather.7.cloned.1.call-done = bf16[1,2,1,512,512]{4,3,2,1,0:T(8,128)(2,1)} async-done(((bf16[1,2,1,128,512]{4,3,2,1,0:T(8,128)(2,1)}), bf16[1,2,1,512,512]{4,3,2,1,0:T(8,128)(2,1)}) %all-gather.7.cloned.1.call-update) | async-done | bytes 1048592 | tf_op jit(solution)/shard_map/all_gather | solution.py:29
  68.6 1.4 fusion.30
  70.0 1.3 fusion.31
  71.3 0.0 copy-done.2
  71.3 0.2 fusion.5
  71.5 0.2 fusion.4
  71.8 0.8 maximum_select_fusion.1
  72.6 0.0 all-reduce.3.cloned.1.call-update
  72.6 56.3 %all-reduce.3.cloned.1.call-done = (f32[2,128,512]{2,1,0:T(8,128)}, f32[2,128,512]{2,1,0:T(8,128)}) async-done(((f32[2,128,512]{2,1,0:T(8,128)}, f32[2,128,512]{2,1,0:T(8,128)}), (f32[2,128,512]{2,1,0:T(8,128)}, f32[2,128,512]{2,1,0:T(8,128)})) %all-reduce.3.cloned.1.call-update) | async-done | bytes 1048592 | tf_op jit(solution)/shard_map/psum | solution.py:9
  128.9 1.3 stack.53
  130.2 52.0 %all_to_all.19 = f32[4,2,128,512]{3,2,1,0:T(8,128)} all-to-all(f32[4,2,128,512]{3,2,1,0:T(8,128)S(1)} %stack.53), channel_id=1, replica_groups=mesh['branch'=8,'mode'=4] {'mode'}, dimensions={0} | all-to-all | bytes 4194304 | tf_op jit(solution)/shard_map/all_to_all | solution.py:40
  182.2 1.6 stack.60
  183.8 3.6 %all-to-all-start.2 = ((f32[4,2,128,512]{3,2,1,0:T(8,128)}), f32[4,2,128,512]{3,2,1,0:T(8,128)S(1)}, u32[]{:S(2)}, u32[]{:S(2)}) async-start(f32[4,2,128,512]{3,2,1,0:T(8,128)} %stack.60), calls=%async_computation.2 | async-start | bytes 4194304 | tf_op jit(solution)/shard_map/all_to_all | solution.py:40
  187.4 3.1 %fusion.50 = (f32[1,1,512,1,512]{4,3,2,1,0:T(1,128)S(1)}, f32[1,1,512,1,512]{4,3,2,1,0:T(1,128)S(1)}) fusion(f32[2,1,512,1,512]{4,3,2,1,0:T(1,128)} %param.4), kind=kLoop, calls=%fused_computation.66 | loop fusion | bytes 4194304 | tf_op jit(solution)/shard_map/slice | solution.py:45
  190.6 0.2 fusion.51
  190.8 3.6 %fusion.18 = f32[512,512]{1,0:T(8,128)S(1)} fusion(f32[512,512]{1,0:T(8,128)S(1)} %bitcast.100, f32[1,1,512,1,512]{4,3,2,1,0:T(1,128)S(1)} %get-tuple-element.12), kind=kOutput, calls=%fused_computation.28 | convolution fusion | flops 1610612736 | bytes 3145728 | tf_op jit(solution)/shard_map/dot_general | solution.py:14
  194.3 3.6 %fusion.3 = f32[1,512,512]{1,2,0:T(8,128)S(1)} fusion(f32[512,512]{1,0:T(8,128)S(1)} %fusion.18, f32[512,512]{1,0:T(8,128)S(1)} %bitcast.102, f32[1,1,512,1,512]{4,3,2,1,0:T(1,128)S(1)} %get-tuple-element.11), kind=kOutput, calls=%fused_computation.9 | convolution fusion | flops 1610874880 | bytes 4194304 | tf_op jit(solution)/shard_map/dot_general | solution.py:14
  197.9 3.6 %fusion.16 = f32[512,512]{1,0:T(8,128)S(1)} fusion(f32[512,512]{1,0:T(8,128)S(1)} %bitcast.103, f32[1,1,512,1,512]{4,3,2,1,0:T(1,128)S(1)} %get-tuple-element.12), kind=kOutput, calls=%fused_computation.26 | convolution fusion | flops 1610612736 | bytes 3145728 | tf_op jit(solution)/shard_map/dot_general | solution.py:17
  201.5 3.7 %fusion.2 = f32[1,512,512]{1,2,0:T(8,128)S(1)} fusion(f32[512,512]{1,0:T(8,128)S(1)} %fusion.16, f32[512,512]{1,0:T(8,128)S(1)} %bitcast.101, f32[1,1,512,1,512]{4,3,2,1,0:T(1,128)S(1)} %get-tuple-element.11), kind=kOutput, calls=%fused_computation.7 | convolution fusion | flops 1610874880 | bytes 4194304 | tf_op jit(solution)/shard_map/dot_general | solution.py:17
  205.2 0.2 maximum_bitcast_fusion
  205.4 2.9 copy.6
  208.3 26.3 %all-to-all-done.2 = f32[4,2,128,512]{3,2,1,0:T(8,128)S(1)} async-done(((f32[4,2,128,512]{3,2,1,0:T(8,128)}), f32[4,2,128,512]{3,2,1,0:T(8,128)S(1)}, u32[]{:S(2)}, u32[]{:S(2)}) %all-to-all-start.2) | async-done | bytes 2097184 | tf_op jit(solution)/shard_map/all_to_all | solution.py:40
  234.6 1.3 copy-done
  235.9 4.5 %all-to-all-start.1 = ((f32[2,1,512,1,512]{2,0,3,1,4:T(2,128)}), f32[2,1,512,1,512]{2,0,3,1,4:T(2,128)}, u32[]{:S(2)}, u32[]{:S(2)}) async-start(f32[2,1,512,1,512]{2,0,3,1,4:T(2,128)} %copy.6), calls=%async_computation.1 | async-start | bytes 4194304 | tf_op jit(solution)/shard_map/all_to_all | solution.py:47
  240.4 1.8 fusion.49
  242.2 46.0 %all-to-all-done.1 = f32[2,1,512,1,512]{2,0,3,1,4:T(2,128)} async-done(((f32[2,1,512,1,512]{2,0,3,1,4:T(2,128)}), f32[2,1,512,1,512]{2,0,3,1,4:T(2,128)}, u32[]{:S(2)}, u32[]{:S(2)}) %all-to-all-start.1) | async-done | bytes 2097184 | tf_op jit(solution)/shard_map/all_to_all | solution.py:47
  288.2 4.0 %fusion.48 = (f32[1,1,512,1,512]{2,0,3,1,4:T(1,128)S(1)}, f32[1,1,512,1,512]{2,0,3,1,4:T(1,128)S(1)}) fusion(f32[2,1,512,1,512]{2,0,3,1,4:T(2,128)} %all-to-all-done.1), kind=kLoop, calls=%fused_computation.64 | loop fusion | bytes 4194304 | tf_op jit(solution)/shard_map/slice | solution.py:50
  292.2 1.9 fusion.12
  294.1 1.9 fusion.10
  295.9 1.9 fusion.1
  297.8 1.9 fusion
  299.7 0.2 maximum_bitcast_fusion.1
  299.9 3.5 %copy.7 = f32[2,1,512,1,512]{4,3,2,1,0:T(1,128)} copy(f32[2,1,512,1,512]{4,2,0,3,1:T(8,128)S(1)} %maximum_bitcast_fusion.1) | data formatting | bytes 4194304 | tf_op jit(solution)/shard_map/broadcast_in_dim | solution.py:51
  (8 shorter events, 0.0 us)
Async XLA Ops:
  6.5 34.5 %copy-start.4 = (bf16[2,2,1,128,512]{4,3,2,1,0:T(8,128)(2,1)S(1)}, bf16[2,2,1,128,512]{4,3,2,1,0:T(8,128)(2,1)}, u32[]{:S(2)}) copy-start(bf16[2,2,1,128,512]{4,3,2,1,0:T(8,128)(2,1)} %param.5) | copy-start | bytes 1572868
  6.5 33.1 %all-gather.5.cloned.1.call-start = ((), (), s32[]{:S(2)}) async-start(), calls=%async_computation.3 | async-start | bytes 1310720 | tf_op jit(solution)/shard_map/all_gather | solution.py:29
  8.5 60.2 %all-gather.7.cloned.1.call-start = ((), (), s32[]{:S(2)}) async-start(), calls=%async_computation.4 | async-start | bytes 1310720 | tf_op jit(solution)/shard_map/all_gather | solution.py:29
  9.2 119.7 %all-reduce.3.cloned.1.call-start = ((), (), s32[]{:S(2)}) async-start(), calls=%async_computation.5 | async-start | bytes 2097152 | tf_op jit(solution)/shard_map/psum | solution.py:9
  39.6 2.7 copy-start.3
  68.6 2.6 copy-start.2
  130.2 52.0 %copy-start.5 = (f32[2,128,512]{2,1,0:T(8,128)S(1)}, f32[2,128,512]{2,1,0:T(8,128)}, u32[]{:S(2)}) copy-start(f32[2,128,512]{2,1,0:T(8,128)} %get-tuple-element.5) | copy-start | bytes 1572868
  183.8 50.8 %all-to-all-start.2 = ((f32[4,2,128,512]{3,2,1,0:T(8,128)}), f32[4,2,128,512]{3,2,1,0:T(8,128)S(1)}, u32[]{:S(2)}, u32[]{:S(2)}) async-start(f32[4,2,128,512]{3,2,1,0:T(8,128)} %stack.60), calls=%async_computation.2 | async-start | bytes 4194304 | tf_op jit(solution)/shard_map/all_to_all | solution.py:40
  187.4 3.1 %copy-start.1 = (f32[4,2,128,512]{3,2,1,0:T(8,128)S(1)}, f32[4,2,128,512]{3,2,1,0:T(8,128)}, u32[]{:S(2)}) copy-start(f32[4,2,128,512]{3,2,1,0:T(8,128)} %all_to_all.19) | copy-start | bytes 6291460
  234.6 1.3 copy-start
  235.9 52.3 %all-to-all-start.1 = ((f32[2,1,512,1,512]{2,0,3,1,4:T(2,128)}), f32[2,1,512,1,512]{2,0,3,1,4:T(2,128)}, u32[]{:S(2)}, u32[]{:S(2)}) async-start(f32[2,1,512,1,512]{2,0,3,1,4:T(2,128)} %copy.6), calls=%async_computation.1 | async-start | bytes 4194304 | tf_op jit(solution)/shard_map/all_to_all | solution.py:47
Sparse Core Ops, SparseCore 0:
  8.9 30.6 all-gather.4
  41.2 27.3 all-gather.6
  72.7 56.1 all-reduce.2
